TPU v7x, 32 devices: a whole 2x2x4 slice. The times are simulated.
32 devices in a mesh: noise: 8 (over z, x), qi: 2 (over core), kj: 2 (over y).
Axes of the slice: x: 2, y: 2, z: 4, core: 2. Of those that a mesh axis runs over, the one named last changes fastest.
Arguments:
- pair_rep: bfloat16 [128, 2, 64, 128], P('qi', None, 'kj'), may hold values from -6 to 6
- query_rows: bfloat16 [8, 128, 768], P('noise', 'qi'), may hold values from -10 to 10
- key_rows: bfloat16 [8, 2, 64, 768], P('noise', None, 'kj'), may hold values from -10 to 10
- value_rows: bfloat16 [8, 2, 64, 768], P('noise', None, 'kj'), may hold values from -6 to 6
- output_grad: bfloat16 [8, 128, 768], P('noise', 'qi'), may hold values from -24 to 24
- gain_first: float32 [128], replicated, may hold values from 0.5 to 1.5
- gate_weight: bfloat16 [128, 512], replicated, may hold values from -0.5 to 0.5
- up_weight: bfloat16 [128, 512], replicated, may hold values from -0.5 to 0.5
- down_weight: bfloat16 [512, 128], replicated, may hold values from -0.25 to 0.25
- gain_second: float32 [128], replicated, may hold values from 0.5 to 1.5
- head_weight: bfloat16 [128, 16], replicated, may hold values from -0.5 to 0.5
Outputs:
- query_grad: bfloat16 [8, 128, 768], P('noise', ('qi', 'kj'))
- key_grad: bfloat16 [8, 128, 768], P('noise', ('qi', 'kj'))
- value_grad: bfloat16 [8, 128, 768], P('noise', ('qi', 'kj'))
- pair_grad: bfloat16 [2, 8, 8, 2, 64, 128], P('qi', 'noise', None, None, 'kj')
- gate_grad: float32 [128, 512], replicated
- up_grad: float32 [128, 512], replicated
- down_grad: float32 [512, 128], replicated
- head_grad: float32 [128, 16], replicated
- first_grad: float32 [128], replicated
- second_grad: float32 [128], replicated
All inputs are finite; a program needn't handle non-finite values.
Results may differ from a plain program's by a relative error of at most 0.011.
Values may be sent and summed in bfloat16 or wider, within the bound.
A program may use at most 64 MiB of HBM per device.

v0:
```python
import jax
import jax.numpy as jnp
from jax import lax
from jax.sharding import PartitionSpec as P

HEADS = 16
HEAD_DIM = 48


epsilon = 1e-05


def merged(value, axis, combine):
    everything = jax.tree.map(lambda part: lax.all_gather(part, axis), value)
    initial = jax.tree.map(lambda part: part[0], everything)

    def hop(k, so_far):
        return combine(so_far, jax.tree.map(lambda part: part[k], everything))

    return lax.fori_loop(1, lax.axis_size(axis), hop, initial)


def layer_norm(values, gain_vec):
    center = values - jnp.mean(values, axis=1, keepdims=True)
    inverse = lax.rsqrt(jnp.mean(center * center, axis=1, keepdims=True) + epsilon)
    normed = center * inverse
    return (normed, inverse, normed * gain_vec)


def norm_backward(normed_grad, normed, inverse):
    first_mean = jnp.mean(normed_grad, axis=1, keepdims=True)
    second_mean = jnp.mean(normed_grad * normed, axis=1, keepdims=True)
    return inverse * (normed_grad - first_mean - normed * second_mean)


def transition_forward(cells, params):
    gain_first, gate_weight, up_weight, down_weight, gain_second, head_weight = params
    inputs = cells.astype(jnp.float32)
    pre_normed, pre_inverse, pre_scaled = layer_norm(inputs, gain_first)
    pre_lowered = pre_scaled.astype(jnp.bfloat16)
    gate_pre = jnp.dot(pre_lowered, gate_weight, preferred_element_type=jnp.float32)
    up_pre = jnp.dot(pre_lowered, up_weight, preferred_element_type=jnp.float32)
    gate_sigmoid = jax.nn.sigmoid(gate_pre)
    hidden = (gate_pre * gate_sigmoid * up_pre).astype(jnp.bfloat16)
    updated = inputs + jnp.dot(hidden, down_weight, preferred_element_type=jnp.float32)
    post_normed, post_inverse, post_scaled = layer_norm(updated, gain_second)
    post_lowered = post_scaled.astype(jnp.bfloat16)
    bias_heads = jnp.einsum(
        "mc,ch->hm", post_lowered, head_weight, preferred_element_type=jnp.float32
    ).astype(jnp.bfloat16)
    saved_state = (
        pre_normed,
        pre_inverse,
        pre_lowered,
        gate_pre,
        up_pre,
        gate_sigmoid,
        hidden,
        post_normed,
        post_inverse,
        post_lowered,
    )
    return (bias_heads, saved_state)


def transition_backward(saved_state, grad_heads, params):
    gain_first, gate_weight, up_weight, down_weight, gain_second, head_weight = params
    (
        pre_normed,
        pre_inverse,
        pre_lowered,
        gate_pre,
        up_pre,
        gate_sigmoid,
        hidden,
        post_normed,
        post_inverse,
        post_lowered,
    ) = saved_state
    grad_low = grad_heads.astype(jnp.bfloat16)
    post_scaled = jnp.einsum("hm,ch->mc", grad_low, head_weight, preferred_element_type=jnp.float32)
    head_part = jnp.einsum("mc,hm->ch", post_lowered, grad_low, preferred_element_type=jnp.float32)
    second_part = jnp.sum(post_scaled * post_normed, axis=0)
    updated_grad = norm_backward(post_scaled * gain_second, post_normed, post_inverse)
    updated_low = updated_grad.astype(jnp.bfloat16)
    down_part = jnp.einsum("mf,mc->fc", hidden, updated_low, preferred_element_type=jnp.float32)
    hidden_grad = jnp.einsum(
        "mc,fc->mf", updated_low, down_weight, preferred_element_type=jnp.float32
    )
    gate_low = (
        hidden_grad * up_pre * gate_sigmoid * (1.0 + gate_pre * (1.0 - gate_sigmoid))
    ).astype(jnp.bfloat16)
    up_low = (hidden_grad * gate_pre * gate_sigmoid).astype(jnp.bfloat16)
    gate_part = jnp.einsum("mc,mf->cf", pre_lowered, gate_low, preferred_element_type=jnp.float32)
    up_part = jnp.einsum("mc,mf->cf", pre_lowered, up_low, preferred_element_type=jnp.float32)
    pre_scaled = jnp.einsum(
        "mf,cf->mc", gate_low, gate_weight, preferred_element_type=jnp.float32
    ) + jnp.einsum("mf,cf->mc", up_low, up_weight, preferred_element_type=jnp.float32)
    first_part = jnp.sum(pre_scaled * pre_normed, axis=0)
    inputs_grad = norm_backward(pre_scaled * gain_first, pre_normed, pre_inverse)
    pair_low = (updated_grad + inputs_grad).astype(jnp.bfloat16)
    return (pair_low, (gate_part, up_part, down_part, head_part, first_part, second_part))


def combine_stats(earlier, later):
    early_max, early_sum, early_dot = earlier
    late_max, late_sum, late_dot = later
    largest = jnp.maximum(early_max, late_max)
    early_scale = jnp.exp(early_max - largest)
    late_scale = jnp.exp(late_max - largest)
    return (
        largest,
        early_sum * early_scale + late_sum * late_scale,
        early_dot * early_scale + late_dot * late_scale,
    )


def local(
    pair_rep,
    query_rows,
    key_rows,
    value_rows,
    output_grad,
    gain_first,
    gate_weight,
    up_weight,
    down_weight,
    gain_second,
    head_weight,
):
    params = (gain_first, gate_weight, up_weight, down_weight, gain_second, head_weight)
    tile_rows, block_count, block_rows, channels = pair_rep.shape
    key_count = block_count * block_rows
    feature_width = query_rows.shape[2]
    score_scale = HEAD_DIM ** (-0.5)
    noise_count = lax.axis_size("noise")
    share_rows = tile_rows // noise_count
    own_start = lax.axis_index("noise") * share_rows
    pair_tile = pair_rep.reshape(tile_rows, key_count, channels)
    own_cells = lax.dynamic_slice_in_dim(pair_tile, own_start, share_rows, 0).reshape(
        share_rows * key_count, channels
    )

    def block_bias(cells):
        return transition_forward(cells, params)[0]

    row_blocks = pair_tile.reshape(noise_count, share_rows * key_count, channels)
    bias_blocks = lax.map(block_bias, row_blocks)
    bias_tile = (
        bias_blocks.reshape(noise_count, HEADS, share_rows, key_count)
        .transpose(1, 3, 0, 2)
        .reshape(HEADS, key_count, tile_rows)
    )
    saved_state = transition_forward(own_cells, params)[1]
    query_tile = query_rows[0].reshape(tile_rows, HEADS, HEAD_DIM)
    keys_tile = key_rows[0].reshape(key_count, HEADS, HEAD_DIM)
    values_tile = value_rows[0].reshape(key_count, HEADS, HEAD_DIM)
    grad_tile = output_grad[0].reshape(tile_rows, HEADS, HEAD_DIM)
    scores = jnp.einsum(
        "qhd,khd->hkq", query_tile, keys_tile, preferred_element_type=jnp.float32
    ) * score_scale + bias_tile.astype(jnp.float32)
    local_max = jnp.max(scores, axis=1)
    local_expo = jnp.exp(scores - local_max[:, None, :])
    attend_grad = jnp.einsum(
        "qhd,khd->hkq", grad_tile, values_tile, preferred_element_type=jnp.float32
    )
    local_sum = jnp.sum(local_expo, axis=1)
    local_dot = jnp.sum(local_expo * attend_grad, axis=1)
    row_max, row_sum, row_dot = merged((local_max, local_sum, local_dot), "kj", combine_stats)
    attend = jnp.exp(scores - row_max[:, None, :]) / row_sum[:, None, :]
    score_grad = attend * (attend_grad - (row_dot / row_sum)[:, None, :])
    score_low = score_grad.astype(jnp.bfloat16)
    attend_low = attend.astype(jnp.bfloat16)
    product = (
        jnp.einsum("hkq,khd->qhd", score_low, keys_tile, preferred_element_type=jnp.float32)
        * score_scale
    )
    query_sum = lax.psum_scatter(
        product.reshape(block_rows * lax.axis_size("kj"), feature_width),
        "kj",
        scatter_dimension=0,
        tiled=True,
    )
    row_count = block_rows * lax.axis_size("qi")
    key_part = (
        jnp.einsum("hkq,qhd->khd", score_low, query_tile, preferred_element_type=jnp.float32)
        * score_scale
    )
    value_part = jnp.einsum(
        "hkq,qhd->khd", attend_low, grad_tile, preferred_element_type=jnp.float32
    )
    key_sum = lax.psum_scatter(
        jnp.concatenate(
            (
                key_part.reshape(row_count, feature_width),
                value_part.reshape(row_count, feature_width),
            ),
            1,
        ),
        "qi",
        scatter_dimension=0,
        tiled=True,
    )
    query_grad = query_sum.astype(jnp.bfloat16)[None]
    key_grad = key_sum[:, :feature_width].astype(jnp.bfloat16)[None]
    value_grad = key_sum[:, feature_width:].astype(jnp.bfloat16)[None]
    summed = lax.psum(score_grad, "noise")
    share_grad = lax.dynamic_slice_in_dim(summed, own_start, share_rows, 2)
    grad_heads = share_grad.transpose(0, 2, 1).reshape(HEADS, share_rows * key_count)
    pair_low, weight_parts = transition_backward(saved_state, grad_heads, params)
    reduced = lax.psum(
        (
            weight_parts[0],
            weight_parts[1],
            weight_parts[2],
            weight_parts[3],
            weight_parts[4],
            weight_parts[5],
        ),
        ("noise", "qi", "kj"),
    )
    tokens = tile_rows * lax.axis_size("qi")
    factor = 1.0 / tokens
    pair_grad = pair_low.reshape(1, 1, share_rows, block_count, block_rows, channels)
    return (
        query_grad,
        key_grad,
        value_grad,
        pair_grad,
        reduced[0] * factor,
        reduced[1] * factor,
        reduced[2] * factor,
        reduced[3] * factor,
        reduced[4] * factor,
        reduced[5] * factor,
    )


def solution(mesh):
    return jax.shard_map(
        local,
        mesh=mesh,
        in_specs=(
            P("qi", None, "kj", None),
            P("noise", "qi", None),
            P("noise", None, "kj", None),
            P("noise", None, "kj", None),
            P("noise", "qi", None),
            P(),
            P(),
            P(),
            P(),
            P(),
            P(),
        ),
        out_specs=(
            P("noise", ("qi", "kj"), None),
            P("noise", ("qi", "kj"), None),
            P("noise", ("qi", "kj"), None),
            P("qi", "noise", None, None, "kj", None),
            P(),
            P(),
            P(),
            P(),
            P(),
            P(),
        ),
        check_vma=False,
    )
```

profile of v0, /device:TPU:0, one launch (start us, length us, event | category | flops | bytes accessed | tf_op | source)
XLA Modules:
  0.0 254.7 jit_solution(7503992493576670872)
XLA Ops:
  8.7 31.2 %while.2 = (s32[]{:T(128)}, bf16[8,16,512]{2,1,0:T(8,128)(2,1)S(1)}, bf16[8,512,128]{2,1,0:T(8,128)(2,1)}, f32[128]{0:T(128)S(1)}, bf16[128,512]{1,0:T(8,128)(2,...) while((s32[]{:T(128)}, ...), condition=%wide.region_5.6_spmd, body=%wide.region_0.5_spmd.sunk | while | flops 206709760 | bytes 5961417 | solution.py:148
  8.7 0.9 constant_dynamic-slice_fusion.2
  12.6 0.9 constant_dynamic-slice_fusion.2
  13.8 0.8 copy-done
  16.5 0.9 constant_dynamic-slice_fusion.2
  20.4 0.9 constant_dynamic-slice_fusion.2
  21.6 0.8 copy-done
  24.3 0.9 constant_dynamic-slice_fusion.2
  25.5 0.8 copy-done
  28.2 0.9 constant_dynamic-slice_fusion.2
  32.1 0.9 constant_dynamic-slice_fusion.2
  36.0 0.9 constant_dynamic-slice_fusion.2
  40.0 0.8 copy-done.12
  43.8 5.3 %all-gather = f32[32,64]{1,0:T(8,128)S(1)} all-gather(f32[16,64]{1,0:T(8,128)S(1)} %get-tuple-element.132), channel_id=2, replica_groups=mesh['noise'=8,'qi'=2,'kj'=2] {'kj'}, dimensions={0}, use_global_device_ids=true | all-gather | bytes 12288 | tf_op jit(solution)/shard_map/all_gather | solution.py:14
  49.8 4.4 %all-gather.2 = f32[32,64]{1,0:T(8,128)S(1)} all-gather(f32[16,64]{1,0:T(8,128)S(1)} %get-tuple-element.93), channel_id=4, replica_groups=mesh['noise'=8,'qi'=2,'kj'=2] {'kj'}, dimensions={0}, use_global_device_ids=true | all-gather | bytes 12288 | tf_op jit(solution)/shard_map/all_gather | solution.py:14
  54.1 4.3 %all-gather.1 = f32[32,64]{1,0:T(8,128)S(1)} all-gather(f32[16,64]{1,0:T(8,128)S(1)} %get-tuple-element.94), channel_id=3, replica_groups=mesh['noise'=8,'qi'=2,'kj'=2] {'kj'}, dimensions={0}, use_global_device_ids=true | all-gather | bytes 12288 | tf_op jit(solution)/shard_map/all_gather | solution.py:14
  58.9 0.8 copy.40
  60.4 1.0 convolution_multiply_fusion.3
  61.5 44.0 %all-reduce.6 = bf16[16,64,64]{2,1,0:T(8,128)(2,1)S(1)} all-reduce(f32[16,64,64]{2,1,0:T(8,128)S(1)} %subtract_multiply_fusion), channel_id=1, replica_groups=mesh['noise'=8,'qi'=2,'kj'=2] {'noise'}, use_global_device_ids=true, to_apply=%region_15.16 | all-reduce | flops 65536 | bytes 393216 | tf_op jit(solution)/shard_map/psum | solution.py:207
  110.6 1.0 fusion.61
  111.5 1.0 fusion.60
  112.5 1.0 fusion.45
  113.6 1.0 fusion.40
  114.7 1.2 copy.44
  115.9 0.8 copy.43
  116.7 1.7 pad_maximum_fusion
  120.1 37.1 %all-reduce = (f32[128,16]{0,1:T(8,128)S(1)}, f32[128]{0:T(128)S(1)}, f32[128]{0:T(128)S(1)}) all-reduce(f32[128,16]{0,1:T(8,128)S(1)} %fusion.44, f32[128]{0:T(128)S(1)} %get-tuple-element.91, f32[128]{0:T(128)S(1)} %get-tuple-element.95), channel_id=1, replica_groups=mesh['noise'=8,'qi'=2,'kj'=2] {'noise','qi','kj'}, use_global_device_ids=true, to_apply=%region_23.24 | all-reduce | flops 2304 | bytes 18432 | tf_op jit(solution)/shard_map/psum | solution.py:211
  158.8 1.0 add_convert_fusion
  159.8 1.5 convert_bitcast_fusion.1
  161.3 80.8 %all-reduce.5.cloned.1.call-done = (f32[128,512]{1,0:T(8,128)}, f32[128,512]{1,0:T(8,128)}, f32[512,128]{1,0:T(8,128)}) async-done(((f32[128,512]{1,0:T(8,128)}, f32[128,512]{1,0:T(8,128)}, f32[512,128]{1,0:T(8,128)}), (f32[128,512]{1,0:T(8,128)}, f32[128,512]{1,0:T(8,128)}, f32[512,128]{1,0:T(8,128)})) %all-reduce.5.cloned.1.call-update) | async-done | bytes 786448 | tf_op jit(solution)/shard_map/psum | solution.py:211
  242.1 1.7 broadcast_multiply_fusion.4
  245.6 0.9 convert.8
  (216 shorter events, 37.4 us)
Async XLA Ops:
  8.0 151.8 %reduce-scatter.3.cloned.1.call-start = ((), (), s32[]{:S(2)}) async-start(), calls=%async_computation.2 | async-start | bytes 294912 | tf_op jit(solution)/shard_map/reduce_scatter | solution.py:178
  9.8 0.9 copy-start
  10.7 1.0 copy-start.9
  13.7 0.9 copy-start
  14.6 0.9 copy-start.7
  14.6 1.0 copy-start.9
  17.6 0.9 copy-start
  18.5 1.0 copy-start.9
  21.5 0.9 copy-start
  22.4 0.9 copy-start.7
  22.4 1.0 copy-start.9
  25.4 0.9 copy-start
  26.3 0.9 copy-start.7
  26.3 1.0 copy-start.9
  29.3 0.9 copy-start
  30.2 1.0 copy-start.9
  33.2 0.9 copy-start
  34.1 0.9 copy-start.7
  34.1 1.0 copy-start.9
  37.1 0.9 copy-start
  38.0 1.0 copy-start.9
  43.5 5.7 %copy-start.15 = (bf16[1,2,32,768]{3,2,1,0:T(8,128)(2,1)S(1)}, bf16[1,2,32,768]{3,2,1,0:T(8,128)(2,1)}, u32[]{:S(2)}) copy-start(bf16[1,2,32,768]{3,2,1,0:T(8,128)(2,1)} %param.16) | copy-start | bytes 294916
  58.6 1.2 copy-start.2
  59.7 182.4 %all-reduce.5.cloned.1.call-start = ((), (), s32[]{:S(2)}) async-start(), calls=%async_computation.4 | async-start | bytes 1572864 | tf_op jit(solution)/shard_map/psum | solution.py:211
  105.9 0.9 copy-start.1
  106.8 0.9 copy-start.10
  107.7 0.9 copy-start.8
  113.6 132.1 %reduce-scatter.5.cloned.1.call-start = ((), (), s32[]{:S(2)}) async-start(), calls=%async_computation.3 | async-start | bytes 589824 | tf_op jit(solution)/shard_map/reduce_scatter | solution.py:192
  114.7 1.2 copy-start.3
  118.7 0.9 copy-start.11
  242.1 1.7 copy-start.5
  243.9 1.0 copy-start.4
  (10 other events, 8.3 us)
Sparse Core Ops, SparseCore 0:
  59.9 12.7 reduce-scatter.2
  118.5 5.9 reduce-scatter.4
Sparse Core Ops, SparseCore 1:
  113.6 128.4 all-reduce.4
where the time goes:
time: 256 us; the launch traced here: 255 us
  blocking collectives  95.1 us (37%)
  waiting for transfers between devices  80.9 us (32%)
  local copies, waits for them, and re-layouts  30.5 us (12%)
  matrix products  19.2 us (8%)
  between operations  15.8 us (6%)
  other arithmetic  12.7 us (5%)
    psum x1, waiting for transfers between devices, local(): lax.psum((weight_parts[0], weight_parts[1], weight_parts[2], weight_parts...  80.8 us
    psum x1, blocking collectives, local(): summed = lax.psum(score_grad, 'noise')  44 us
    psum x1, blocking collectives, local(): lax.psum((weight_parts[0], weight_parts[1], weight_parts[2], weight_parts...  37.1 us
    all_gather x3, blocking collectives, merged(): everything = jax.tree.map(lambda part: lax.all_gather(part, axis), value)  14 us
    while x48, local copies, waits for them, and re-layouts  10.9 us
    dynamic_slice x16, local copies, waits for them, and re-layouts, local(): bias_blocks = lax.map(block_bias, row_blocks)  8.23 us
    dot_general x9, matrix products, transition_forward(): jnp.dot(hidden, down_weight, preferred_element_type=jnp.float32)  5.96 us
    unnamed x30, local copies, waits for them, and re-layouts  5.75 us
  transfers between devices with their start and end apart: 3, of which 1 were waited for; matrix products, arithmetic and copies ran while one was open for 8% of the time, Pallas kernels for 0%

commit v1 on v0

v1 whole, which is shorter than its diff:
```python
import functools

import jax
import jax.numpy as jnp
from jax import lax
from jax.experimental import pallas as pl
from jax.experimental.pallas import tpu as pltpu
from jax.sharding import PartitionSpec as P

HEADS = 16
HEAD_DIM = 48
ALIGN = 16

epsilon = 1e-05
F32 = jnp.float32
BF16 = jnp.bfloat16
MESH = pl.DeviceIdType.MESH


def dot(left, right, left_dim, right_dim):
    return lax.dot_general(
        left, right, (((left_dim,), (right_dim,)), ((), ())), preferred_element_type=F32
    )


def normalize(values):
    center = values - jnp.mean(values, axis=1, keepdims=True)
    inverse = lax.rsqrt(jnp.mean(center * center, axis=1, keepdims=True) + epsilon)
    return center * inverse, inverse


def norm_backward(normed_grad, normed, inverse):
    first_mean = jnp.mean(normed_grad, axis=1, keepdims=True)
    second_mean = jnp.mean(normed_grad * normed, axis=1, keepdims=True)
    return inverse * (normed_grad - first_mean - normed * second_mean)


def kernel(
    sizes,
    pair_ref,
    q_ref,
    k_ref,
    v_ref,
    g_ref,
    gain_first_ref,
    gate_ref,
    up_ref,
    down_ref,
    gain_second_ref,
    head_ref,
    query_out,
    key_out,
    value_out,
    pair_out,
    weight_out,
    cells,
    pre_normed,
    pre_low,
    pre_low_t,
    gate_coef,
    up_coef,
    hidden,
    hidden_t,
    post_normed,
    post_low,
    inverses,
    bias_rows,
    bias_all,
    score,
    attend_grad,
    stats,
    grad_send,
    grad_recv,
    grad_sum,
    post_scaled,
    query_part,
    query_recv,
    kv_part,
    kv_recv,
    w_part,
    w_core,
    w_sum,
    w_recv,
    cell_sem,
    bias_send_sem,
    bias_recv_sem,
    stat_send_sem,
    stat_recv_sem,
    grad_send_sem,
    grad_recv_sem,
    query_send_sem,
    query_recv_sem,
    pair_sems,
    w_send_sem,
    w_recv_sem,
    all_send_sem,
    all_recv_sem,
    fwd_send_sem,
    fwd_recv_sem,
):
    n_noise, n_qi, n_kj, rows, keys, share, block = sizes
    group = n_noise * n_kj
    cell_count = share * keys
    chunk = min(256, cell_count)
    scale = HEAD_DIM ** (-0.5)
    noise = lax.axis_index("noise")
    qi = lax.axis_index("qi")
    kj = lax.axis_index("kj")
    me = noise * n_kj + kj
    sibling = {"qi": 1 - qi}
    channels = cells.shape[-1]
    width = q_ref.shape[-1]
    half = keys // n_qi
    q_half = rows // n_kj

    def remote(src, dst, send, recv, device):
        return pltpu.make_async_remote_copy(
            src_ref=src, dst_ref=dst, send_sem=send, recv_sem=recv, device_id=device, device_id_type=MESH
        )

    def of_group(index):
        return {"noise": index // n_kj, "kj": lax.rem(index, n_kj)}

    def each(count, body):
        def step(i, carry):
            body(i)
            return carry

        lax.fori_loop(1, count, step, 0)

    own = pltpu.make_async_copy(pair_ref.at[pl.ds(noise * share, share)], cells, cell_sem)
    own.start()

    barrier = pltpu.get_barrier_semaphore()

    def greet(i):
        pl.semaphore_signal(
            barrier, inc=1, device_id=of_group(lax.rem(me + i, group)), device_id_type=MESH
        )

    each(group, greet)
    pl.semaphore_signal(barrier, inc=1, device_id=sibling, device_id_type=MESH)
    own.wait()

    gain_first = gain_first_ref[...]
    gain_second = gain_second_ref[...]
    head_t = head_ref[...].astype(F32).T.astype(BF16)
    flat_cells = cells[...].reshape(cell_count, channels)
    for start in range(0, cell_count, chunk):
        at = slice(start, start + chunk)
        inputs = flat_cells[at].astype(F32)
        normed, inverse = normalize(inputs)
        lowered = (normed * gain_first).astype(BF16)
        gate_pre = dot(lowered, gate_ref[...], 1, 0)
        up_pre = dot(lowered, up_ref[...], 1, 0)
        sigmoid = jax.nn.sigmoid(gate_pre)
        silu = gate_pre * sigmoid
        low_hidden = (silu * up_pre).astype(BF16)
        updated = inputs + dot(low_hidden, down_ref[...], 1, 0)
        after, after_inverse = normalize(updated)
        after_low = (after * gain_second).astype(BF16)
        pre_normed[at] = normed
        pre_low[at] = lowered
        gate_coef[at] = up_pre * sigmoid * (1.0 + gate_pre * (1.0 - sigmoid))
        up_coef[at] = silu
        hidden[at] = low_hidden
        post_normed[at] = after
        post_low[at] = after_low
        inverses[at, 0:1] = inverse
        inverses[at, 1:2] = after_inverse
    for i in range(share):
        bias_rows[i] = dot(head_t, post_low[i * keys : (i + 1) * keys], 1, 1)
    for h in range(HEADS):
        bias_all[noise, h] = bias_rows[:, h, :].astype(BF16)

    pl.semaphore_wait(barrier, group)

    def bias_copy(slot, peer):
        return remote(
            bias_all.at[slot], bias_all.at[slot], bias_send_sem.at[peer], bias_recv_sem.at[slot], {"noise": peer}
        )

    each(n_noise, lambda i: bias_copy(noise, lax.rem(noise + i, n_noise)).start())

    def head_of(ref, h):
        return ref[:, h * HEAD_DIM : (h + 1) * HEAD_DIM]

    for h in range(HEADS):
        score[h] = dot(head_of(q_ref, h), head_of(k_ref, h), 1, 1) * scale
        attend_grad[h] = dot(head_of(g_ref, h), head_of(v_ref, h), 1, 1)

    def bias_wait(i):
        peer = lax.rem(noise + n_noise - i, n_noise)
        bias_copy(peer, peer).wait_recv()

    each(n_noise, bias_wait)

    for h in range(HEADS):
        full = score[h] + bias_all[:, h].astype(F32).reshape(rows, keys)
        largest = jnp.max(full, axis=1, keepdims=True)
        expo = jnp.exp(full - largest)
        score[h] = expo
        stats[kj, :, h : h + 1] = largest
        stats[kj, :, HEADS + h : HEADS + h + 1] = jnp.sum(expo, axis=1, keepdims=True)
        stats[kj, :, 2 * HEADS + h : 2 * HEADS + h + 1] = jnp.sum(
            expo * attend_grad[h], axis=1, keepdims=True
        )

    def stat_copy(slot, peer):
        return remote(
            stats.at[slot], stats.at[slot], stat_send_sem.at[peer], stat_recv_sem.at[slot], {"kj": peer}
        )

    each(n_kj, lambda i: stat_copy(kj, lax.rem(kj + i, n_kj)).start())
    hidden_t[...] = hidden[...].T
    pre_low_t[...] = pre_low[...].T

    def stat_wait(i):
        peer = lax.rem(kj + n_kj - i, n_kj)
        stat_copy(peer, peer).wait_recv()

    each(n_kj, stat_wait)

    parts = [stats[j] for j in range(n_kj)]
    row_max = parts[0][:, 0:HEADS]
    for part in parts[1:]:
        row_max = jnp.maximum(row_max, part[:, 0:HEADS])
    row_sum = jnp.zeros_like(row_max)
    row_dot = jnp.zeros_like(row_max)
    for part in parts:
        weight = jnp.exp(part[:, 0:HEADS] - row_max)
        row_sum += weight * part[:, HEADS : 2 * HEADS]
        row_dot += weight * part[:, 2 * HEADS : 3 * HEADS]
    factor = jnp.exp(stats[kj, :, 0:HEADS] - row_max) / row_sum
    delta = row_dot / row_sum
    for h in range(HEADS):
        attend = score[h] * factor[:, h : h + 1]
        score_grad = attend * (attend_grad[h] - delta[:, h : h + 1])
        score[h] = attend
        attend_grad[h] = score_grad
        grad_send[:, h] = score_grad.reshape(n_noise, share, keys).astype(BF16)

    def grad_copy(slot, peer):
        return remote(
            grad_send.at[peer], grad_recv.at[slot], grad_send_sem.at[peer], grad_recv_sem.at[slot], {"noise": peer}
        )

    each(n_noise, lambda i: grad_copy(noise, lax.rem(noise + i, n_noise)).start())

    for h in range(HEADS):
        at = slice(h * HEAD_DIM, (h + 1) * HEAD_DIM)
        value_at = slice(width + h * HEAD_DIM, width + (h + 1) * HEAD_DIM)
        score_low = attend_grad[h].astype(BF16)
        attend_low = score[h].astype(BF16)
        query_part[:, :, at] = (
            (dot(score_low, head_of(k_ref, h), 1, 0) * scale).astype(BF16).reshape(n_kj, q_half, HEAD_DIM)
        )
        kv_part[:, :, at] = (
            (dot(score_low, head_of(q_ref, h), 0, 0) * scale).astype(BF16).reshape(n_qi, half, HEAD_DIM)
        )
        kv_part[:, :, value_at] = (
            dot(attend_low, head_of(g_ref, h), 0, 0).astype(BF16).reshape(n_qi, half, HEAD_DIM)
        )

    def query_copy(slot, peer):
        return remote(
            query_part.at[peer], query_recv.at[slot], query_send_sem.at[peer], query_recv_sem.at[slot], {"kj": peer}
        )

    each(n_kj, lambda i: query_copy(kj, lax.rem(kj + i, n_kj)).start())
    kv_copy = remote(kv_part.at[1 - qi], kv_recv, pair_sems.at[0], pair_sems.at[1], sibling)
    kv_copy.start()

    def grad_wait(i):
        peer = lax.rem(noise + n_noise - i, n_noise)
        grad_copy(peer, peer).wait_recv()

    grad_sum[...] = grad_send[noise].astype(F32)

    def grad_add(i):
        grad_wait(i)
        peer = lax.rem(noise + n_noise - i, n_noise)
        grad_sum[...] += grad_recv[peer].astype(F32)

    each(n_noise, grad_add)

    head_part = jnp.zeros((HEADS, channels), F32)
    for i in range(share):
        at = slice(i * keys, (i + 1) * keys)
        grad_low = grad_sum[:, i, :].astype(BF16)
        post_scaled[at] = dot(grad_low, head_t, 0, 0)
        head_part += dot(grad_low, post_low[at], 1, 0)
    hidden_count = gate_ref.shape[1]
    tiles = hidden_count // channels
    first_part = jnp.zeros((1, channels), F32)
    second_part = jnp.zeros((1, channels), F32)
    down_part = jnp.zeros((hidden_count, channels), F32)
    gate_part = jnp.zeros((channels, hidden_count), F32)
    up_part = jnp.zeros((channels, hidden_count), F32)
    for start in range(0, cell_count, chunk):
        at = slice(start, start + chunk)
        scaled = post_scaled[at]
        after = post_normed[at]
        second_part += jnp.sum(scaled * after, axis=0, keepdims=True)
        updated_grad = norm_backward(scaled * gain_second, after, inverses[at, 1:2])
        updated_low = updated_grad.astype(BF16)
        down_part += dot(hidden_t[:, at], updated_low, 1, 0)
        hidden_grad = dot(updated_low, down_ref[...], 1, 1)
        gate_low = (hidden_grad * gate_coef[at]).astype(BF16)
        up_low = (hidden_grad * up_coef[at]).astype(BF16)
        gate_part += dot(pre_low_t[:, at], gate_low, 1, 0)
        up_part += dot(pre_low_t[:, at], up_low, 1, 0)
        pre_scaled = dot(gate_low, gate_ref[...], 1, 1) + dot(up_low, up_ref[...], 1, 1)
        normed = pre_normed[at]
        first_part += jnp.sum(pre_scaled * normed, axis=0, keepdims=True)
        inputs_grad = norm_backward(pre_scaled * gain_first, normed, inverses[at, 0:1])
        pair_out[at] = (updated_grad + inputs_grad).astype(BF16)

    for t in range(tiles):
        at = slice(t * channels, (t + 1) * channels)
        w_part[at] = gate_part[:, at].astype(BF16)
        w_part[hidden_count + t * channels : hidden_count + (t + 1) * channels] = up_part[:, at].astype(BF16)
    w_part[2 * hidden_count : 3 * hidden_count] = down_part.astype(BF16)
    tail = 3 * hidden_count
    w_part[tail : tail + HEADS] = head_part.astype(BF16)
    w_part[tail + HEADS : tail + 2 * HEADS] = jnp.concatenate(
        (
            jnp.broadcast_to(first_part, (HEADS // 2, channels)),
            jnp.broadcast_to(second_part, (HEADS // 2, channels)),
        ),
        0,
    ).astype(BF16)
    if w_part.shape[0] > tail + 2 * HEADS:
        w_part[tail + 2 * HEADS :] = jnp.zeros((w_part.shape[0] - tail - 2 * HEADS, channels), BF16)

    span = group * block

    def half_rows(index):
        return pl.ds(pl.multiple_of(index * span, ALIGN), span)

    core_copy = remote(w_part.at[half_rows(1 - qi)], w_core, pair_sems.at[2], pair_sems.at[3], sibling)
    core_copy.start()

    total = query_part[kj].astype(F32)

    def query_add(i, total):
        peer = lax.rem(kj + n_kj - i, n_kj)
        query_copy(peer, peer).wait_recv()
        return total + query_recv[peer].astype(F32)

    query_out[...] = lax.fori_loop(1, n_kj, query_add, total).astype(BF16)
    kv_copy.wait_recv()
    kv_total = kv_part[qi].astype(F32) + kv_recv[...].astype(F32)
    key_out[...] = kv_total[:, :width].astype(BF16)
    value_out[...] = kv_total[:, width:].astype(BF16)

    core_copy.wait_recv()
    w_sum[...] = (w_part[half_rows(qi)].astype(F32) + w_core[...].astype(F32)).astype(BF16)

    def own_rows(index):
        return pl.ds(pl.multiple_of(index * block, ALIGN), block)

    def w_copy(slot, peer):
        return remote(
            w_sum.at[own_rows(peer)], w_recv.at[slot], w_send_sem.at[peer], w_recv_sem.at[slot], of_group(peer)
        )

    each(group, lambda i: w_copy(me, lax.rem(me + i, group)).start())

    def w_add(i, total):
        peer = lax.rem(me + group - i, group)
        w_copy(peer, peer).wait_recv()
        return total + w_recv[peer].astype(F32)

    total = lax.fori_loop(1, group, w_add, w_sum[own_rows(me)].astype(F32))

    def out_rows(core, index):
        return pl.ds(pl.multiple_of((core * group + index) * block, ALIGN), block)

    mine = out_rows(qi, me)
    weight_out[mine] = (total * (1.0 / (rows * n_qi))).astype(BF16)

    def all_copy(slot, peer):
        at = out_rows(qi, slot)
        return remote(weight_out.at[at], weight_out.at[at], all_send_sem.at[peer], all_recv_sem.at[slot], of_group(peer))

    def fwd_copy(core, slot):
        at = out_rows(core, slot)
        return remote(weight_out.at[at], weight_out.at[at], fwd_send_sem.at[slot], fwd_recv_sem.at[slot], sibling)

    each(group, lambda i: all_copy(me, lax.rem(me + i, group)).start())
    fwd_copy(qi, me).start()

    def forward(i):
        peer = lax.rem(me + group - i, group)
        all_copy(peer, peer).wait_recv()
        fwd_copy(qi, peer).start()

    each(group, forward)

    def fwd_wait(i, carry):
        fwd_copy(1 - qi, i).wait_recv()
        fwd_copy(qi, i).wait_send()
        return carry

    lax.fori_loop(0, group, fwd_wait, 0)

    def drain(i):
        peer = lax.rem(me + i, group)
        w_copy(me, peer).wait_send()
        all_copy(me, peer).wait_send()

    each(group, drain)

    def drain_noise(i):
        peer = lax.rem(noise + i, n_noise)
        bias_copy(noise, peer).wait_send()
        grad_copy(noise, peer).wait_send()

    each(n_noise, drain_noise)

    def drain_kj(i):
        peer = lax.rem(kj + i, n_kj)
        stat_copy(kj, peer).wait_send()
        query_copy(kj, peer).wait_send()

    each(n_kj, drain_kj)
    kv_copy.wait_send()
    core_copy.wait_send()


def finish(hidden_count, weight_ref, gate_out, up_out, down_out, head_out, first_out, second_out):
    channels = weight_ref.shape[1]
    for t in range(hidden_count // channels):
        at = slice(t * channels, (t + 1) * channels)
        gate_out[:, at] = weight_ref[at].astype(F32)
        up_out[:, at] = weight_ref[hidden_count + t * channels : hidden_count + (t + 1) * channels].astype(F32)
    down_out[...] = weight_ref[2 * hidden_count : 3 * hidden_count].astype(F32)
    tail = 3 * hidden_count
    head_out[...] = weight_ref[tail : tail + HEADS].astype(F32).T
    small = weight_ref[tail + HEADS : tail + 2 * HEADS].astype(F32)
    first_out[...] = small[0:1]
    second_out[...] = small[HEADS // 2 : HEADS // 2 + 1]


def local(
    mesh_shape,
    pair_rep,
    query_rows,
    key_rows,
    value_rows,
    output_grad,
    gain_first,
    gate_weight,
    up_weight,
    down_weight,
    gain_second,
    head_weight,
):
    n_noise, n_qi, n_kj = mesh_shape
    rows, block_count, block_rows, channels = pair_rep.shape
    keys = block_count * block_rows
    width = query_rows.shape[2]
    share = rows // n_noise
    count = share * keys
    group = n_noise * n_kj
    hidden_count = gate_weight.shape[1]
    total_rows = 3 * hidden_count + 2 * HEADS
    block = -(-total_rows // (n_qi * group * ALIGN)) * ALIGN
    half = keys // n_qi
    q_half = rows // n_kj
    sizes = (n_noise, n_qi, n_kj, rows, keys, share, block)
    vmem = pl.BlockSpec(memory_space=pltpu.VMEM)
    dma = pltpu.SemaphoreType.DMA
    span = n_qi * group * block

    scratch = [
        pltpu.VMEM((share, block_count, block_rows, channels), BF16),
        pltpu.VMEM((count, channels), F32),
        pltpu.VMEM((count, channels), BF16),
        pltpu.VMEM((channels, count), BF16),
        pltpu.VMEM((count, hidden_count), F32),
        pltpu.VMEM((count, hidden_count), F32),
        pltpu.VMEM((count, hidden_count), BF16),
        pltpu.VMEM((hidden_count, count), BF16),
        pltpu.VMEM((count, channels), F32),
        pltpu.VMEM((count, channels), BF16),
        pltpu.VMEM((count, 128), F32),
        pltpu.VMEM((share, HEADS, keys), F32),
        pltpu.VMEM((n_noise, HEADS, share, keys), BF16),
        pltpu.VMEM((HEADS, rows, keys), F32),
        pltpu.VMEM((HEADS, rows, keys), F32),
        pltpu.VMEM((n_kj, rows, 128), F32),
        pltpu.VMEM((n_noise, HEADS, share, keys), BF16),
        pltpu.VMEM((n_noise, HEADS, share, keys), BF16),
        pltpu.VMEM((HEADS, share, keys), F32),
        pltpu.VMEM((count, channels), F32),
        pltpu.VMEM((n_kj, q_half, width), BF16),
        pltpu.VMEM((n_kj, q_half, width), BF16),
        pltpu.VMEM((n_qi, half, 2 * width), BF16),
        pltpu.VMEM((half, 2 * width), BF16),
        pltpu.VMEM((span, channels), BF16),
        pltpu.VMEM((group * block, channels), BF16),
        pltpu.VMEM((group * block, channels), BF16),
        pltpu.VMEM((group, block, channels), BF16),
        dma(()),
        dma((n_noise,)),
        dma((n_noise,)),
        dma((n_kj,)),
        dma((n_kj,)),
        dma((n_noise,)),
        dma((n_noise,)),
        dma((n_kj,)),
        dma((n_kj,)),
        dma((4,)),
        dma((group,)),
        dma((group,)),
        dma((group,)),
        dma((group,)),
        dma((group,)),
        dma((group,)),
    ]
    query_grad, key_grad, value_grad, pair_grad, weights = pl.pallas_call(
        functools.partial(kernel, sizes),
        out_shape=(
            jax.ShapeDtypeStruct((q_half, width), BF16),
            jax.ShapeDtypeStruct((half, width), BF16),
            jax.ShapeDtypeStruct((half, width), BF16),
            jax.ShapeDtypeStruct((count, channels), BF16),
            jax.ShapeDtypeStruct((span, channels), BF16),
        ),
        in_specs=[pl.BlockSpec(memory_space=pl.ANY)] + [vmem] * 10,
        out_specs=(vmem,) * 5,
        scratch_shapes=scratch,
        compiler_params=pltpu.CompilerParams(
            collective_id=0, has_side_effects=True, vmem_limit_bytes=60 * 1024 * 1024
        ),
        name="block_backward",
    )(
        pair_rep,
        query_rows.reshape(rows, width),
        key_rows.reshape(keys, width),
        value_rows.reshape(keys, width),
        output_grad.reshape(rows, width),
        gain_first.reshape(1, channels),
        gate_weight,
        up_weight,
        down_weight,
        gain_second.reshape(1, channels),
        head_weight,
    )
    gate_grad, up_grad, down_grad, head_grad, first_grad, second_grad = pl.pallas_call(
        functools.partial(finish, hidden_count),
        out_shape=(
            jax.ShapeDtypeStruct((channels, hidden_count), F32),
            jax.ShapeDtypeStruct((channels, hidden_count), F32),
            jax.ShapeDtypeStruct((hidden_count, channels), F32),
            jax.ShapeDtypeStruct((channels, HEADS), F32),
            jax.ShapeDtypeStruct((1, channels), F32),
            jax.ShapeDtypeStruct((1, channels), F32),
        ),
        in_specs=[vmem],
        out_specs=(vmem,) * 6,
        name="finish_weights",
    )(weights)
    return (
        query_grad[None],
        key_grad[None],
        value_grad[None],
        pair_grad.reshape(1, 1, share, block_count, block_rows, channels),
        gate_grad,
        up_grad,
        down_grad,
        head_grad,
        first_grad.reshape(channels),
        second_grad.reshape(channels),
    )


def solution(mesh):
    mesh_shape = (mesh.shape["noise"], mesh.shape["qi"], mesh.shape["kj"])
    return jax.shard_map(
        functools.partial(local, mesh_shape),
        mesh=mesh,
        in_specs=(
            P("qi", None, "kj", None),
            P("noise", "qi", None),
            P("noise", None, "kj", None),
            P("noise", None, "kj", None),
            P("noise", "qi", None),
            P(),
            P(),
            P(),
            P(),
            P(),
            P(),
        ),
        out_specs=(
            P("noise", ("qi", "kj"), None),
            P("noise", ("qi", "kj"), None),
            P("noise", ("qi", "kj"), None),
            P("qi", "noise", None, None, "kj", None),
            P(),
            P(),
            P(),
            P(),
            P(),
            P(),
        ),
        check_vma=False,
    )
```

time: 256 us -> 54.1 us (0.21)
  blocking collectives: 95.1 us -> 0 us
  waiting for transfers between devices: 80.9 us -> 0 us
  Pallas kernels: 0 us -> 47.1 us
  local copies, waits for them, and re-layouts: 30.5 us -> 5.64 us
  matrix products: 19.2 us -> 0 us
  between operations: 15.8 us -> 0.67 us
  other arithmetic: 12.7 us -> 0 us
    psum x2 -> x0, blocking collectives: 81.1 us -> none  [the longest x1 44 us: local(): summed = lax.psum(score_grad, 'noise')]
    psum x1 -> x0, waiting for transfers between devices: 80.8 us -> none  [local(): lax.psum((weight_parts[0], weight_parts[1], weight_parts[2], weight_parts...]
    pallas_call x0 -> x2, Pallas kernels: none -> 47.1 us  [the longest x1 45.1 us: local(): pl.pallas_call(functools.partial(kernel, sizes), out_shape=(jax.ShapeDtyp...]
    dot_general x40 -> x0, matrix products: 19.2 us -> none  [the longest x9 5.96 us: transition_forward(): jnp.dot(hidden, down_weight, preferred_element_type=jnp.float32)]
    all_gather x3 -> x0, blocking collectives: 14 us -> none  [merged(): everything = jax.tree.map(lambda part: lax.all_gather(part, axis), value)]
    while x48 -> x0, local copies, waits for them, and re-layouts: 10.9 us -> none
    dynamic_slice x16 -> x0, local copies, waits for them, and re-layouts: 8.23 us -> none  [local(): bias_blocks = lax.map(block_bias, row_blocks)]
    mul x8 -> x0, other arithmetic: 5.26 us -> none  [the longest x1 1.72 us: local(): reduced[0] * factor]
  transfers between devices with their start and end apart: 3 -> 0, of which waited for: 1 -> 0; matrix products, arithmetic and copies ran while one was open for 8% -> 0% of each run, Pallas kernels for 0% -> 0%
where the time goes in v1:
time: 54.1 us; the launch traced here: 53.4 us
  Pallas kernels  47.1 us (87%)
  local copies, waits for them, and re-layouts  5.64 us (10%)
  between operations  0.67 us (1%)
    pallas_call x1, Pallas kernels, local(): pl.pallas_call(functools.partial(kernel, sizes), out_shape=(jax.ShapeDtyp...  45.1 us
    unnamed x16, local copies, waits for them, and re-layouts  5.64 us
    pallas_call x1, Pallas kernels, local(): pl.pallas_call(functools.partial(finish, hidden_count), out_shape=(jax.Sh...  1.97 us

profile of v1, /device:TPU:0, one launch (start us, length us, event | category | flops | bytes accessed | tf_op | source)
XLA Modules:
  0.0 53.4 jit_solution(9127317415367645818)
XLA Ops:
  0.6 0.0 copy-start.4
  0.7 0.7 %copy-done.4 = bf16[128,16]{0,1:T(8,128)(2,1)S(1)} copy-done((bf16[128,16]{0,1:T(8,128)(2,1)S(1)}, bf16[128,16]{0,1:T(8,128)(2,1)}, u32[]{:S(2)}) %copy-start.4) | copy-done | bytes 4120
  1.3 0.7 %copy.21.head_ref = bf16[128,16]{1,0:T(8,128)(2,1)} copy(bf16[128,16]{0,1:T(8,128)(2,1)S(1)} %copy-done.4) | data formatting | bytes 8192 | tf_op args[10]
  2.1 45.1 %block_backward.1 = (bf16[32,768]{1,0:T(8,128)(2,1)}, bf16[32,768]{1,0:T(8,128)(2,1)}, bf16[32,768]{1,0:T(8,128)(2,1)}, bf16[512,128]{1,0:T(8,128)(2,1)}, bf16[2048,128]{1,0:T(8,128)(2,1)}) custom-call(bf16[64,2,32,128]{3,2,1,0:T(8,128)(2,1)} %pair_ref.1, bf16[64,768]{1,0:T(8,128)(2,1)} %bitcast.13, bf16[64,768]{1,0:T(8,128)(2,1)} %bitcast.14, ...), custom_call_target="tpu_custom_call" | custom-call | tf_op jit(solution)/shard_map/block_backward/pallas_call | solution.py:523
  47.1 2.0 %finish_weights.1 = (f32[128,512]{1,0:T(8,128)}, f32[128,512]{1,0:T(8,128)}, f32[512,128]{1,0:T(8,128)}, f32[128,16]{1,0:T(8,128)}, f32[1,128]{1,0:T(1,128)}, /*index=5*/f32[1,128]{1,0:T(1,128)}) custom-call(bf16[2048,128]{1,0:T(8,128)(2,1)} %get-tuple-element.25.weight_ref), custom_call_target="tpu_custom_call" | custom-call | tf_op jit(solution)/shard_map/finish_weights/pallas_call | solution.py:552
  49.1 0.0 copy-start.3
  49.1 0.0 copy-start.2
  49.1 1.5 %copy.22 = f32[128,16]{0,1:T(8,128)} copy(f32[128,16]{1,0:T(8,128)} %get-tuple-element.39) | data formatting | bytes 16384
  50.6 0.0 copy-done.3
  50.6 0.0 copy-start
  50.6 0.6 %copy.27 = bf16[1,32,768]{2,1,0:T(8,128)(2,1)} copy(bf16[1,32,768]{2,1,0:T(8,128)(2,1)S(1)} %bitcast.19) | data formatting | bytes 98304
  51.3 0.0 copy-done.2
  51.3 0.0 copy-start.1
  51.3 0.6 %copy.28 = bf16[1,32,768]{2,1,0:T(8,128)(2,1)} copy(bf16[1,32,768]{2,1,0:T(8,128)(2,1)S(1)} %bitcast.18) | data formatting | bytes 98304
  51.9 0.2 copy-done.1
  52.1 0.6 %copy.29 = bf16[1,32,768]{2,1,0:T(8,128)(2,1)} copy(bf16[1,32,768]{2,1,0:T(8,128)(2,1)S(1)} %bitcast.17) | data formatting | bytes 98304
  52.7 0.0 copy-done
  52.7 0.7 %copy.30 = bf16[1,1,8,2,32,128]{5,4,3,2,1,0:T(8,128)(2,1)} copy(bf16[1,1,8,2,32,128]{5,4,3,2,1,0:T(8,128)(2,1)S(1)} %bitcast.12) | data formatting | bytes 262144
Async XLA Ops:
  0.6 0.7 %copy-start.4 = (bf16[128,16]{0,1:T(8,128)(2,1)S(1)}, bf16[128,16]{0,1:T(8,128)(2,1)}, u32[]{:S(2)}) copy-start(bf16[128,16]{0,1:T(8,128)(2,1)} %param.21) | copy-start | bytes 12292
  49.1 1.5 %copy-start.3 = (bf16[32,768]{1,0:T(8,128)(2,1)S(1)}, bf16[32,768]{1,0:T(8,128)(2,1)}, u32[]{:S(2)}) copy-start(bf16[32,768]{1,0:T(8,128)(2,1)} %get-tuple-element.21) | copy-start | bytes 147460
  49.1 2.1 %copy-start.2 = (bf16[32,768]{1,0:T(8,128)(2,1)S(1)}, bf16[32,768]{1,0:T(8,128)(2,1)}, u32[]{:S(2)}) copy-start(bf16[32,768]{1,0:T(8,128)(2,1)} %get-tuple-element.22) | copy-start | bytes 147460
  50.6 2.1 %copy-start = (bf16[512,128]{1,0:T(8,128)(2,1)S(1)}, bf16[512,128]{1,0:T(8,128)(2,1)}, u32[]{:S(2)}) copy-start(bf16[512,128]{1,0:T(8,128)(2,1)} %get-tuple-element.24) | copy-start | bytes 393220
  51.3 0.8 %copy-start.1 = (bf16[32,768]{1,0:T(8,128)(2,1)S(1)}, bf16[32,768]{1,0:T(8,128)(2,1)}, u32[]{:S(2)}) copy-start(bf16[32,768]{1,0:T(8,128)(2,1)} %get-tuple-element.23) | copy-start | bytes 147460
